TPU v7x, 32 devices: a whole 2x2x4 slice. The times are simulated.
32 devices in a mesh: seq: 8 (over y, x, core), head: 4 (over z).
Axes of the slice: x: 2, y: 2, z: 4, core: 2. Of those that a mesh axis runs over, the one named last changes fastest.
Arguments:
- hidden_in: float32 [4096, 768], P('seq'), may hold values from -6 to 6
- grad_out: float32 [4096, 768], P('seq'), may hold values from -6 to 6
- doc_lengths: int32 [3], replicated, may hold values from 1 to 2048, as said below
- norm_gain: float32 [2, 768], replicated, may hold values from 0.5 to 1.5
- proj_z: float32 [2, 768, 1536], P(None, 'seq', 'head'), may hold values from -0.21875 to 0.21875
- proj_x: float32 [2, 768, 1536], P(None, 'seq', 'head'), may hold values from -0.21875 to 0.21875
- proj_bc: float32 [2, 768, 256], P(None, 'seq', 'head'), may hold values from -0.21875 to 0.21875
- proj_dt: float32 [2, 768, 24], P(None, 'seq', 'head'), may hold values from -0.21875 to 0.21875
- conv_x_kernel: float32 [2, 4, 1536], P(None, None, 'head'), may hold values from -3 to 3
- conv_x_bias: float32 [2, 1536], P(None, 'head'), may hold values from -0.5 to 0.5
- conv_bc_kernel: float32 [2, 4, 256], P(None, None, 'head'), may hold values from -3 to 3
- conv_bc_bias: float32 [2, 256], P(None, 'head'), may hold values from -0.5 to 0.5
- dt_bias: float32 [2, 24], P(None, 'head'), may hold values from -6 to -3
- a_log: float32 [2, 24], P(None, 'head'), may hold values from -3 to 2
- skip_gain: float32 [2, 24], P(None, 'head'), may hold values from 0.5 to 1.5
- gate_gain: float32 [2, 1536], P(None, 'head'), may hold values from 0.5 to 1.5
- proj_out: float32 [2, 768, 1536], P(None, 'seq', 'head'), may hold values from -0.15625 to 0.15625
Outputs:
- hidden_out: float32 [4096, 768], P('seq')
- grad_hidden: float32 [4096, 768], P('seq')
- grad_norm_gain: float32 [2, 768], replicated
- grad_proj_z: float32 [2, 768, 1536], P(None, 'seq', 'head')
- grad_proj_x: float32 [2, 768, 1536], P(None, 'seq', 'head')
- grad_proj_bc: float32 [2, 768, 256], P(None, 'seq', 'head')
- grad_proj_dt: float32 [2, 768, 24], P(None, 'seq', 'head')
- grad_conv_x_kernel: float32 [2, 4, 1536], P(None, None, 'head')
- grad_conv_x_bias: float32 [2, 1536], P(None, 'head')
- grad_conv_bc_kernel: float32 [2, 4, 256], P(None, None, 'head')
- grad_conv_bc_bias: float32 [2, 256], P(None, 'head')
- grad_dt_bias: float32 [2, 24], P(None, 'head')
- grad_a_log: float32 [2, 24], P(None, 'head')
- grad_skip_gain: float32 [2, 24], P(None, 'head')
- grad_gate_gain: float32 [2, 1536], P(None, 'head')
- grad_proj_out: float32 [2, 768, 1536], P(None, 'seq', 'head')
Inputs may be any that keep to these rules, and one draw needn't show every extreme that they name: `doc_lengths`: the 3 lengths sum to 4096, and the longest is exactly 2048.
All inputs are finite; a program needn't handle non-finite values.
Results may differ from a plain program's by a relative error of at most 0.0003.
Values sent between devices are 32-bit elements; how exact they have to be, the bound alone decides.
A program may use at most 192 MiB of HBM per device.

v0:
```python
from functools import partial
import jax
import jax.numpy as jnp
from jax import lax
from jax.sharding import PartitionSpec as P

STATE = 128
KERNEL = 4
BLOCK = 256
EPS = 1e-05
NEG_FILL = -1e30
EXACT = lax.Precision.HIGHEST
FAST = lax.Precision.HIGH


def passed_along(array, axis, by):
    count = lax.axis_size(axis)
    pairs = [(i, i + by) for i in range(count) if 0 <= i + by < count]
    return lax.ppermute(array, axis, pairs)


def product(spec, left, right, precision=FAST):
    return jnp.einsum(spec, left, right, precision=precision, preferred_element_type=jnp.float32)


def swish_act(values):
    return values * jax.nn.sigmoid(values)


def rms_scale(values):
    return lax.rsqrt(jnp.mean(values * values, axis=-1, keepdims=True) + EPS)


def segment_ids(doc_lengths, positions):
    ends = jnp.cumsum(doc_lengths)
    starts = ends - doc_lengths
    return jnp.sum((positions[:, None] >= starts[None, :]).astype(jnp.int32), axis=1) - 1


def widened(per_head, width):
    heads = per_head.shape[1]
    owner = jnp.arange(width) // (width // heads)
    spread = (jnp.arange(heads)[:, None] == owner[None, :]).astype(jnp.float32)
    return product("th,hc->tc", per_head, spread, EXACT)


def scaled_heads(state, factors):
    heads = factors.shape[0]
    return (state.reshape(heads, -1, state.shape[-1]) * factors[:, None, None]).reshape(state.shape)


def entering(pieces, decays, backward):
    count, mine = (lax.axis_size("seq"), lax.axis_index("seq"))
    order = jnp.arange(count)
    first, middle = (order[:, None], order[None, :])
    if backward:
        between = (middle > mine) & (middle < first)
        outside = order > mine
    else:
        between = (middle > first) & (middle < mine)
        outside = order < mine
    weights = jnp.prod(jnp.where(between[..., None], decays[None], 1.0), axis=1)
    weights = jnp.where(outside[:, None], weights, 0.0)
    heads = decays.shape[1]
    split = pieces.reshape(count, heads, -1, pieces.shape[-1])
    return jnp.sum(split * weights[:, :, None, None], axis=0).reshape(pieces.shape[1:])


def with_rows(rows, extra):
    width = rows.shape[1]
    more = -(-extra.shape[0] // (8 * width)) * 8
    return jnp.concatenate(
        [rows, jnp.pad(extra, (0, more * width - extra.shape[0])).reshape(more, width)], axis=0
    )


def front_fn(hidden, gain, weight_zx, weight_bd, inner_loc):
    normed = hidden * rms_scale(hidden) * gain[None, :]
    main = product("td,dc->tc", normed, weight_zx)
    side = product("td,dc->tc", normed, weight_bd)
    raw = jnp.concatenate([main[:, inner_loc:], side[:, : 2 * STATE]], axis=1)
    return (main[:, :inner_loc], raw, side[:, 2 * STATE :])


def conv_local(raw, prev_tail, kernel, bias, keeps):
    extended = jnp.concatenate([prev_tail, raw], axis=0)
    count = raw.shape[0]
    total = jnp.zeros_like(raw) + bias[None, :]
    for offset in range(KERNEL):
        total = total + kernel[offset][None, :] * extended[offset : offset + count] * keeps[offset]
    return swish_act(total)


def local_fn(values, dt_raw, dt_bias, a_log, skip_gain, bc, seg_now, seg_prev):
    count, width = values.shape
    heads = dt_raw.shape[1]
    rows = min(BLOCK, count)
    blocks = count // rows
    step_size = jax.nn.softplus(dt_raw + dt_bias)
    log_decay = -step_size * jnp.exp(a_log)
    order = jnp.arange(rows)
    lower = order[:, None] >= order[None, :]
    cum = product(
        "ts,bsh->bth", lower.astype(jnp.float32), log_decay.reshape(blocks, rows, heads), EXACT
    )
    cum_rows = cum.transpose(2, 0, 1)
    seg = seg_now.reshape(blocks, rows)
    before = jnp.concatenate([seg_prev[None], seg[:-1, -1]])
    allowed = lower[None] & (seg[:, :, None] == seg[:, None, :])
    spans = cum_rows[:, :, :, None] - cum_rows[:, :, None, :]
    decays = jnp.exp(jnp.where(allowed[None], spans, NEG_FILL))
    b_matrix = bc[:, :STATE].reshape(blocks, rows, STATE)
    c_matrix = bc[:, STATE:].reshape(blocks, rows, STATE)
    scores = decays * product("btn,bsn->bts", c_matrix, b_matrix)[None]
    stepped = values * widened(step_size, width)
    output = product(
        "hbts,bshp->bthp", scores, stepped.reshape(blocks, rows, heads, width // heads)
    ).reshape(count, width)
    output = output + jnp.repeat(skip_gain, width // heads)[None, :] * values
    last = cum[:, -1]
    enter = jnp.exp(cum) * (seg == before[:, None]).astype(jnp.float32)[..., None]
    keep_end = (seg == seg[:, -1:]).astype(jnp.float32)
    leave = jnp.exp(last[:, None] - cum) * keep_end[..., None]
    weighted = stepped * widened(leave.reshape(count, heads), width)
    states = product("bsc,bsn->bcn", weighted.reshape(blocks, rows, width), b_matrix)
    carries = jnp.exp(last) * (seg[:, -1] == before).astype(jnp.float32)[:, None]
    state, decay = (states[0], carries[0])
    for block in range(1, blocks):
        state = scaled_heads(state, carries[block]) + states[block]
        decay = decay * carries[block]
    return (output, enter.reshape(count, heads), states, carries, state, decay)


def mix_fn(output, enter, states, carries, state_in, bc):
    count, width = output.shape
    blocks = states.shape[0]
    entry = [state_in]
    for block in range(blocks - 1):
        entry.append(scaled_heads(entry[-1], carries[block]) + states[block])
    c_matrix = bc[:, STATE:].reshape(blocks, count // blocks, STATE)
    read = product("btn,bcn->btc", c_matrix, jnp.stack(entry)).reshape(count, width)
    return output + widened(enter, width) * read


def gate_fn(mixed, gate_in, gate_gain, proj_out_loc):
    gated = mixed * swish_act(gate_in)
    rows = product("tc,dc->td", gated * gate_gain[None, :], proj_out_loc)
    return (rows, jnp.sum(gated * gated, axis=1))


def body(
    hidden_in,
    grad_out,
    doc_lengths,
    norm_gain,
    proj_z,
    proj_x,
    proj_bc,
    proj_dt,
    conv_x_kernel,
    conv_x_bias,
    conv_bc_kernel,
    conv_bc_bias,
    dt_bias,
    a_log,
    skip_gain,
    gate_gain,
    proj_out,
):
    count, width = hidden_in.shape
    layers, rows_loc, inner_loc = proj_z.shape
    bc_loc = proj_bc.shape[2]
    heads = proj_dt.shape[2]
    inner = inner_loc * lax.axis_size("head")
    bc_all = 2 * STATE
    margin = KERNEL - 1
    positions = lax.axis_index("seq") * count + jnp.arange(-margin, count, dtype=jnp.int32)
    seg_ext = segment_ids(doc_lengths, positions)
    seg_now = seg_ext[margin:]
    seg_prev = seg_ext[margin - 1]
    keeps = [
        (seg_ext[offset : offset + count] == seg_now).astype(jnp.float32)[:, None]
        for offset in range(KERNEL)
    ]

    def over_seq(part):
        return lax.all_gather(part, "seq", axis=0, tiled=True)

    columns = lax.all_gather(
        jnp.concatenate([proj_bc, conv_bc_kernel, conv_bc_bias[:, None]], axis=1),
        "head",
        axis=2,
        tiled=True,
    )
    first = over_seq(
        jnp.concatenate(
            [proj_z[0], proj_x[0]]
            + [
                part
                for layer in range(layers)
                for part in (columns[layer, :rows_loc], proj_dt[layer])
            ],
            axis=1,
        )
    )
    rest = over_seq(
        jnp.concatenate(
            [proj_out[0]]
            + [
                part
                for layer in range(1, layers)
                for part in (proj_z[layer], proj_x[layer], proj_out[layer])
            ],
            axis=1,
        )
    )
    full_zx = [first[:, : 2 * inner_loc]]
    full_out = [rest[:, :inner_loc]]
    for layer in range(1, layers):
        at = (3 * layer - 2) * inner_loc
        full_zx.append(rest[:, at : at + 2 * inner_loc])
        full_out.append(rest[:, at + 2 * inner_loc : at + 3 * inner_loc])
    side = first[:, 2 * inner_loc :]
    side_width = bc_all + heads
    full_bd = [side[:, layer * side_width : (layer + 1) * side_width] for layer in range(layers)]
    hidden = hidden_in
    saved = []
    for layer in range(layers):
        front_out, pull_front = jax.vjp(
            partial(front_fn, inner_loc=inner_loc),
            hidden,
            norm_gain[layer],
            full_zx[layer],
            full_bd[layer],
        )
        gate_in, raw, dt_raw = front_out
        prev_tail = passed_along(raw[count - margin :], "seq", 1)
        kernel = jnp.concatenate(
            [conv_x_kernel[layer], columns[layer, rows_loc : rows_loc + KERNEL]], axis=1
        )
        bias = jnp.concatenate([conv_x_bias[layer], columns[layer, rows_loc + KERNEL]])
        conv_out, pull_conv = jax.vjp(
            partial(conv_local, keeps=keeps), raw, prev_tail, kernel, bias
        )
        values, bc = (conv_out[:, :inner_loc], conv_out[:, inner_loc:])
        local_out, pull_local = jax.vjp(
            partial(local_fn, seg_now=seg_now, seg_prev=seg_prev),
            values,
            dt_raw,
            dt_bias[layer],
            a_log[layer],
            skip_gain[layer],
            bc,
        )
        output, enter, states, carries, state_dev, decay_dev = local_out
        packed = jnp.concatenate(
            [state_dev, jnp.pad(decay_dev[None], ((0, 7), (0, STATE - heads)))], axis=0
        )
        pieces = lax.all_gather(packed, "seq")
        decays = pieces[:, inner_loc, :heads]
        state_in = entering(pieces[:, :inner_loc], decays, False)
        mixed, pull_mix = jax.vjp(mix_fn, output, enter, states, carries, state_in, bc)
        (rows, squares), pull_gate = jax.vjp(
            gate_fn, mixed, gate_in, gate_gain[layer], full_out[layer]
        )
        if layer < layers - 1:
            summed = lax.psum(with_rows(rows, squares), "head")
            total_sq = summed[count:].reshape(-1)[:count]
            scale = lax.rsqrt(total_sq / inner + EPS)
            sums = summed[:count]
            hidden = hidden + scale[:, None] * sums
            grad_scale = sums
        else:
            pair = lax.psum(jnp.stack([squares, jnp.sum(grad_out * rows, axis=1)]), "head")
            total_sq, grad_scale = (pair[0], pair[1])
            scale = lax.rsqrt(total_sq / inner + EPS)
            last_rows = scale[:, None] * rows
        saved.append(
            (
                pull_front,
                pull_conv,
                pull_local,
                pull_mix,
                pull_gate,
                scale,
                grad_scale,
                decays,
                state_in,
            )
        )
    grad_hidden = grad_out
    big, small = ([None] * layers for _ in range(2))
    own_bc = []
    for layer in reversed(range(layers)):
        (
            pull_front,
            pull_conv,
            pull_local,
            pull_mix,
            pull_gate,
            scale,
            grad_scale,
            decays,
            state_in,
        ) = saved[layer]
        if layer < layers - 1:
            grad_scale = jnp.sum(grad_hidden * grad_scale, axis=1)
        grad_squares = grad_scale * (-0.5 / inner) * scale * scale * scale
        grad_mixed, grad_gate_in, grad_ggain, grad_full_out = pull_gate(
            (scale[:, None] * grad_hidden, grad_squares)
        )
        grad_output, grad_enter, grad_states, grad_carries, grad_state_in, mix_bc = pull_mix(
            grad_mixed
        )
        grad_pieces = lax.all_gather(grad_state_in, "seq")
        if layer == layers - 1:
            grad_pieces, last_rows = lax.optimization_barrier((grad_pieces, last_rows))
            hidden_out = hidden + lax.psum(last_rows, "head")
        grad_state_end = entering(grad_pieces, decays, True)
        grad_decay = jnp.sum((grad_state_end * state_in).reshape(heads, -1), axis=1)
        grad_values, grad_dt_raw, grad_dbias, grad_alog, grad_skip, local_bc = pull_local(
            (grad_output, grad_enter, grad_states, grad_carries, grad_state_end, grad_decay)
        )
        grad_raw, grad_prev, grad_kernel, grad_cbias = pull_conv(
            jnp.concatenate([grad_values, mix_bc + local_bc], axis=1)
        )
        from_right = passed_along(grad_prev, "seq", -1)
        grad_raw = grad_raw + jnp.pad(from_right, ((count - margin, 0), (0, 0)))
        grad_part, grad_ngain, grad_zx, grad_bd = pull_front((grad_gate_in, grad_raw, grad_dt_raw))
        shared = jnp.concatenate(
            [grad_ngain, grad_kernel[:, inner_loc:].reshape(-1), grad_cbias[inner_loc:]]
        )
        if layer == layers - 1:
            grad_part, hidden_out = lax.optimization_barrier((grad_part, hidden_out))
        summed = lax.psum(with_rows(grad_part, shared), "head")
        grad_hidden = grad_hidden + summed[:count]
        shared = summed[count:].reshape(-1)[: shared.shape[0]]
        big[layer] = lax.psum_scatter(
            jnp.concatenate([grad_full_out, grad_zx, grad_bd], axis=1),
            "seq",
            scatter_dimension=0,
            tiled=True,
        )
        own_bc.append(
            lax.psum_scatter(
                big[layer][:, 3 * inner_loc : 3 * inner_loc + bc_all],
                "head",
                scatter_dimension=1,
                tiled=True,
            )
        )
        small[layer] = (
            grad_kernel[:, :inner_loc].reshape(-1),
            grad_cbias[:inner_loc],
            grad_ggain,
            grad_dbias,
            grad_alog,
            grad_skip,
            shared[:width],
            shared[width : width + KERNEL * bc_all],
            shared[width + KERNEL * bc_all :],
        )

    def laid_out(parts):
        sizes = [part.shape[0] for part in parts[0]]
        stacked = jnp.stack([jnp.concatenate(layer_parts) for layer_parts in parts])
        return (stacked, sizes)

    def taken(stacked, sizes):
        starts = [sum(sizes[:place]) for place in range(len(sizes))]
        return [stacked[:, start : start + size] for start, size in zip(starts, sizes)]

    stacked, sizes = laid_out(small)
    cxk, cxb, ggain, dbias, alog, skip, ngain, cbk, cbb = taken(lax.psum(stacked, "seq"), sizes)
    offset = lax.axis_index("head") * bc_loc
    cbk = lax.dynamic_slice_in_dim(cbk.reshape(layers, KERNEL, bc_all), offset, bc_loc, axis=2)
    cbb = lax.dynamic_slice_in_dim(cbb, offset, bc_loc, axis=1)
    return (
        hidden_out,
        grad_hidden,
        ngain,
        jnp.stack([part[:, inner_loc : 2 * inner_loc] for part in big]),
        jnp.stack([part[:, 2 * inner_loc : 3 * inner_loc] for part in big]),
        jnp.stack(own_bc[::-1]),
        jnp.stack([part[:, 3 * inner_loc + bc_all :] for part in big]),
        cxk.reshape(layers, KERNEL, inner_loc),
        cxb,
        cbk,
        cbb,
        dbias,
        alog,
        skip,
        ggain,
        jnp.stack([part[:, :inner_loc] for part in big]),
    )


def solution(mesh):
    in_specs = (
        P("seq", None),
        P("seq", None),
        P(),
        P(),
        P(None, "seq", "head"),
        P(None, "seq", "head"),
        P(None, "seq", "head"),
        P(None, "seq", "head"),
        P(None, None, "head"),
        P(None, "head"),
        P(None, None, "head"),
        P(None, "head"),
        P(None, "head"),
        P(None, "head"),
        P(None, "head"),
        P(None, "head"),
        P(None, "seq", "head"),
    )
    out_specs = (
        P("seq", None),
        P("seq", None),
        P(),
        P(None, "seq", "head"),
        P(None, "seq", "head"),
        P(None, "seq", "head"),
        P(None, "seq", "head"),
        P(None, None, "head"),
        P(None, "head"),
        P(None, None, "head"),
        P(None, "head"),
        P(None, "head"),
        P(None, "head"),
        P(None, "head"),
        P(None, "head"),
        P(None, "seq", "head"),
    )
    return jax.shard_map(body, mesh=mesh, in_specs=in_specs, out_specs=out_specs, check_vma=False)
```

profile of v0, /device:TPU:0, one launch (start us, length us, event | category | flops | bytes accessed | tf_op | source)
XLA Modules:
  0.0 822.2 jit_solution(18058968250045826087)
XLA Ops:
  10.9 15.7 %all_gather.29 = f32[2,101,256]{1,0,2:T(2,128)S(1)} all-gather(f32[2,101,64]{1,0,2:T(2,128)S(1)} %pad_maximum_fusion.19), channel_id=1, replica_groups=mesh['seq'=8,'head'=4] {'head'}, dimensions={2}, use_global_device_ids=true | all-gather | bytes 258560 | tf_op jit(solution)/shard_map/all_gather | solution.py:189
  34.5 4.4 slice_reduce_fusion.1
  42.0 25.6 %all-gather.9.cloned.1.call-done = f32[768,1292]{1,0:T(8,128)} async-done(((f32[96,1292]{1,0:T(8,128)}), f32[768,1292]{1,0:T(8,128)}) %all-gather.9.cloned.1.call-update) | async-done | bytes 3969040 | tf_op jit(solution)/shard_map/all_gather | solution.py:187
  102.4 3.1 fusion.70
  107.2 17.9 %all-gather.17.cloned.1.call-done = f32[3136,128]{1,0:T(8,128)} async-done(((f32[392,128]{1,0:T(8,128)}), f32[3136,128]{1,0:T(8,128)}) %all-gather.17.cloned.1.call-update) | async-done | bytes 1605648 | tf_op jit(solution)/shard_map/all_gather | solution.py:259
  133.5 4.0 multiply_reduce_fusion.23
  137.5 28.3 %all-gather.11.cloned.1.call-done = f32[768,1536]{1,0:T(8,128)} async-done(((f32[96,1536]{1,0:T(8,128)}), f32[768,1536]{1,0:T(8,128)}) %all-gather.11.cloned.1.call-update) | async-done | bytes 4718608 | tf_op jit(solution)/shard_map/all_gather | solution.py:187
  165.8 3.7 fusion.94
  173.0 67.9 %all-reduce.58.cloned.1.call-done = f32[520,768]{1,0:T(8,128)} async-done(((f32[520,768]{1,0:T(8,128)}), f32[520,768]{1,0:T(8,128)}) %all-reduce.58.cloned.1.call-update) | async-done | bytes 1597456 | tf_op jit(solution)/shard_map/psum | solution.py:267
  250.4 3.9 fusion.18
  268.3 3.3 fusion.316
  287.7 3.3 fusion.76
  292.6 15.9 %all-gather.19.cloned.1.call-done = f32[3136,128]{1,0:T(8,128)} async-done(((f32[392,128]{1,0:T(8,128)}), f32[3136,128]{1,0:T(8,128)}) %all-gather.19.cloned.1.call-update) | async-done | bytes 1605648 | tf_op jit(solution)/shard_map/all_gather | solution.py:259
  324.7 3.9 multiply_reduce_fusion.22
  328.6 4.9 multiply_reduce_fusion.7
  334.2 12.4 %psum.43 = f32[2,512]{1,0:T(2,128)} all-reduce(f32[2,512]{1,0:T(2,128)} %pad_maximum_fusion.25), channel_id=1, replica_groups=mesh['seq'=8,'head'=4] {'head'}, use_global_device_ids=true, to_apply=%region_12.14 | all-reduce | flops 1024 | bytes 8192 | tf_op jit(solution)/shard_map/psum | solution.py:274
  347.4 3.2 fusion.62
  350.6 3.4 multiply_reduce_fusion.18
  374.9 5.3 fusion.25
  420.7 4.9 fusion.89
  425.6 35.7 %all-reduce.60.cloned.1.call-done = f32[512,768]{1,0:T(8,128)} async-done(((f32[512,768]{1,0:T(8,128)}), f32[512,768]{1,0:T(8,128)}) %all-reduce.60.cloned.1.call-update) | async-done | bytes 1572880 | tf_op jit(solution)/shard_map/psum | solution.py:318
  461.3 8.4 %multiply_reduce_fusion.4 = (f32[768]{0:T(1024)S(1)}, f32[512]{0:T(512)S(1)}, f32[512,768]{1,0:T(8,128)}, f32[512,768]{1,0:T(8,128)S(1)}) fusion(f32[512,768]{1,0:T(8,128)S(1)} %get-tuple-element.205, f32[512]{0:T(512)S(1)} %fusion.283, f32[768]{0:T(1024)S(1)} %copy-done.112, f32[512,768]{1,0:T(8,128)} %all-reduce.60.cloned.1.call-done, ...), kind=kOutput, calls=%fused_computation.58 | convolution fusion | flops 1815476992 | bytes 11806720 | tf_op jit(solution)/shard_map/transpose(jvp(td,dc->tc))/dot_general | solution.py:23
  474.2 69.0 %all-reduce.62.cloned.1.call-done = f32[520,768]{1,0:T(8,128)} async-done(((f32[520,768]{1,0:T(8,128)}), f32[520,768]{1,0:T(8,128)}) %all-reduce.62.cloned.1.call-update) | async-done | bytes 1597456 | tf_op jit(solution)/shard_map/psum | solution.py:335
  569.6 5.9 copy.495
  581.0 5.3 fusion.27
  624.5 4.4 multiply_reduce_fusion.1
  640.6 6.0 copy.493
  654.0 62.4 %all-reduce.64.cloned.1.call-done = f32[520,768]{1,0:T(8,128)} async-done(((f32[520,768]{1,0:T(8,128)}), f32[520,768]{1,0:T(8,128)}) %all-reduce.64.cloned.1.call-update) | async-done | bytes 1597456 | tf_op jit(solution)/shard_map/psum | solution.py:335
  717.2 23.5 %psum.47 = f32[2,4370]{1,0:T(2,128)S(1)} all-reduce(f32[2,4370]{1,0:T(2,128)S(1)} %pad_maximum_fusion.21), channel_id=1, replica_groups=mesh['seq'=8,'head'=4] {'seq'}, use_global_device_ids=true, to_apply=%region_65.67 | all-reduce | flops 8740 | bytes 69920 | tf_op jit(solution)/shard_map/psum | solution.py:374
  747.5 25.1 %reduce-scatter.13.cloned.1.call-done = f32[96,1414]{1,0:T(8,128)} async-done(((f32[768,1414]{1,0:T(8,128)}), f32[96,1414]{1,0:T(8,128)}) %reduce-scatter.13.cloned.1.call-update) | async-done | bytes 542992
  780.0 14.4 %reduce-scatter.11.cloned.1.call-done = f32[96,64]{0,1:T(8,128)} async-done(((f32[96,256]{0,1:T(8,128)}), f32[96,64]{0,1:T(8,128)}) %reduce-scatter.11.cloned.1.call-update) | async-done | bytes 24592 | tf_op jit(solution)/shard_map/reduce_scatter | solution.py:345
  794.3 19.8 %reduce-scatter.9.cloned.1.call-done = f32[96,64]{0,1:T(8,128)} async-done(((f32[96,256]{0,1:T(8,128)}), f32[96,64]{0,1:T(8,128)}) %reduce-scatter.9.cloned.1.call-update) | async-done | bytes 24592 | tf_op jit(solution)/shard_map/reduce_scatter | solution.py:345
  (878 shorter events, 290.1 us)
Async XLA Ops:
  7.2 60.3 %all-gather.9.cloned.1.call-start = ((), (), s32[]{:S(2)}) async-start(), calls=%async_computation.4 | async-start | bytes 4866048 | tf_op jit(solution)/shard_map/all_gather | solution.py:187
  28.7 96.4 %all-gather.17.cloned.1.call-start = ((), (), s32[]{:S(2)}) async-start(), calls=%async_computation.14 | async-start | bytes 1806336 | tf_op jit(solution)/shard_map/all_gather | solution.py:259
  32.3 48.5 %copy-start.143 = (f32[640]{0:T(1024)}, f32[640]{0:T(1024)S(1)}, u32[]{:S(2)}) copy-start(f32[640]{0:T(1024)S(1)} %get-tuple-element.174) | copy-start | bytes 7684
  32.3 48.5 %copy-start.145 = (f32[640]{0:T(1024)}, f32[640]{0:T(1024)S(1)}, u32[]{:S(2)}) copy-start(f32[640]{0:T(1024)S(1)} %get-tuple-element.175) | copy-start | bytes 7684
  32.3 48.5 %copy-start.147 = (f32[640]{0:T(1024)}, f32[640]{0:T(1024)S(1)}, u32[]{:S(2)}) copy-start(f32[640]{0:T(1024)S(1)} %get-tuple-element.177) | copy-start | bytes 7684
  32.3 48.5 %copy-start.149 = (f32[640]{0:T(1024)}, f32[640]{0:T(1024)S(1)}, u32[]{:S(2)}) copy-start(f32[640]{0:T(1024)S(1)} %get-tuple-element.176) | copy-start | bytes 7684
  33.7 37.2 %copy-start.106 = (s32[384]{0:T(512)}, s32[384]{0:T(512)S(1)}, u32[]{:S(2)}) copy-start(s32[384]{0:T(512)S(1)} %add_select_fusion) | copy-start | bytes 4612
  40.4 37.9 %copy-start.201 = (f32[2]{0:T(128)}, f32[2]{0:T(128)S(1)}, u32[]{:S(2)}) copy-start(f32[2]{0:T(128)S(1)} %fusion.284) | copy-start | bytes 28
  41.9 36.4 %copy-start.195 = (f32[2,256]{1,0:T(2,128)}, f32[2,256]{1,0:T(2,128)S(1)}, u32[]{:S(2)}) copy-start(f32[2,256]{1,0:T(2,128)S(1)} %get-tuple-element.272) | copy-start | bytes 6148
  42.0 38.9 %copy-start.121 = (f32[512]{0:T(512)}, f32[512]{0:T(512)S(1)}, u32[]{:S(2)}) copy-start(f32[512]{0:T(512)S(1)} %get-tuple-element.268) | copy-start | bytes 6148
  42.0 38.9 %copy-start.123 = (f32[512]{0:T(512)}, f32[512]{0:T(512)S(1)}, u32[]{:S(2)}) copy-start(f32[512]{0:T(512)S(1)} %get-tuple-element.269) | copy-start | bytes 6148
  42.0 38.9 %copy-start.126 = (f32[512]{0:T(512)}, f32[512]{0:T(512)S(1)}, u32[]{:S(2)}) copy-start(f32[512]{0:T(512)S(1)} %get-tuple-element.270) | copy-start | bytes 6148
  76.1 4.2 collective-permute-start
  94.1 71.7 %all-gather.11.cloned.1.call-start = ((), (), s32[]{:S(2)}) async-start(), calls=%async_computation.5 | async-start | bytes 5308416 | tf_op jit(solution)/shard_map/all_gather | solution.py:187
  97.2 143.7 %all-reduce.58.cloned.1.call-start = ((), (), s32[]{:S(2)}) async-start(), calls=%async_computation.6 | async-start | bytes 3194880 | tf_op jit(solution)/shard_map/psum | solution.py:267
  98.8 67.0 %copy-start.160 = (f32[384]{0:T(512)}, f32[384]{0:T(512)S(1)}, u32[]{:S(2)}) copy-start(f32[384]{0:T(512)S(1)} %get-tuple-element.185) | copy-start | bytes 4612
  99.6 283.5 %copy-start.113 = (pred[2,256,256]{2,1,0:T(8,128)(4,1)}, pred[2,256,256]{2,1,0:T(8,128)(4,1)S(1)}, u32[]{:S(2)}) copy-start(pred[2,256,256]{2,1,0:T(8,128)(4,1)S(1)} %compare_and_fusion) | copy-start | bytes 393220
  170.8 137.6 %all-gather.19.cloned.1.call-start = ((), (), s32[]{:S(2)}) async-start(), calls=%async_computation.15 | async-start | bytes 1806336 | tf_op jit(solution)/shard_map/all_gather | solution.py:259
  256.6 3.4 collective-permute-start.1
  278.2 111.5 %all-gather.13.cloned.1.call-start = ((), (), s32[]{:S(2)}) async-start(), calls=%async_computation.7 | async-start | bytes 1769472 | tf_op jit(solution)/shard_map/all_gather | solution.py:315
  362.5 98.8 %all-reduce.60.cloned.1.call-start = ((), (), s32[]{:S(2)}) async-start(), calls=%async_computation.8 | async-start | bytes 3145728 | tf_op jit(solution)/shard_map/psum | solution.py:318
  394.9 148.3 %all-reduce.62.cloned.1.call-start = ((), (), s32[]{:S(2)}) async-start(), calls=%async_computation.9 | async-start | bytes 3194880 | tf_op jit(solution)/shard_map/psum | solution.py:335
  413.5 5.6 collective-permute-start.2
  474.0 72.7 %copy-start.167 = (f32[512]{0:T(512)S(1)}, f32[512]{0:T(512)}, u32[]{:S(2)}) copy-start(f32[512]{0:T(512)} %copy-done.166) | copy-start | bytes 6148
  474.0 120.1 %all-gather.15.cloned.1.call-start = ((), (), s32[]{:S(2)}) async-start(), calls=%async_computation.10 | async-start | bytes 1769472 | tf_op jit(solution)/shard_map/all_gather | solution.py:315
  559.6 90.3 %reduce-scatter.15.cloned.1.call-start = ((), (), s32[]{:S(2)}) async-start(), calls=%async_computation.17 | async-start | bytes 5308416
  575.6 140.8 %all-reduce.64.cloned.1.call-start = ((), (), s32[]{:S(2)}) async-start(), calls=%async_computation.11 | async-start | bytes 3194880 | tf_op jit(solution)/shard_map/psum | solution.py:335
  616.9 4.6 collective-permute-start.3
  630.5 142.1 %reduce-scatter.13.cloned.1.call-start = ((), (), s32[]{:S(2)}) async-start(), calls=%async_computation.16 | async-start | bytes 5308416
  646.7 70.4 %copy-start.218 = (f32[384]{0:T(512)S(1)}, f32[384]{0:T(512)}, u32[]{:S(2)}) copy-start(f32[384]{0:T(512)} %get-tuple-element.215) | copy-start | bytes 4612
  646.7 147.6 %reduce-scatter.11.cloned.1.call-start = ((), (), s32[]{:S(2)}) async-start(), calls=%async_computation.13 | async-start | bytes 163840 | tf_op jit(solution)/shard_map/reduce_scatter | solution.py:345
  653.9 160.2 %reduce-scatter.9.cloned.1.call-start = ((), (), s32[]{:S(2)}) async-start(), calls=%async_computation.12 | async-start | bytes 163840 | tf_op jit(solution)/shard_map/reduce_scatter | solution.py:345
  (239 other events, 1052.9 us)
Sparse Core Ops, SparseCore 0:
  28.8 38.6 all-gather.8
  94.3 30.8 all-gather.16
  127.0 38.7 all-gather.10
  170.9 69.9 all-reduce.57
  278.4 30.0 all-gather.18
  362.6 22.7 all-gather.12
  395.1 66.2 all-reduce.59
  474.1 69.0 all-reduce.61
  559.7 24.6 all-gather.14
  587.7 56.1 reduce-scatter.14
  646.4 69.9 all-reduce.63
  719.6 52.8 reduce-scatter.12
  774.8 19.4 reduce-scatter.10
  796.4 17.6 reduce-scatter.8
where the time goes:
time: 834 us; the launch traced here: 822 us
  waiting for transfers between devices  382 us (46%)
  matrix products  136 us (16%)
  local copies, waits for them, and re-layouts  131 us (16%)
  other arithmetic  94.6 us (11%)
  blocking collectives  51.5 us (6%)
  between operations  17.4 us (2%)
  starting transfers between devices  9.89 us (1%)
    dot_general x58, matrix products, product(): jnp.einsum(spec, left, right, precision=precision, preferred_element_type...  136 us
    psum x2, waiting for transfers between devices, body(): summed = lax.psum(with_rows(grad_part, shared), 'head')  131 us
    psum x1, waiting for transfers between devices, body(): summed = lax.psum(with_rows(rows, squares), 'head')  67.9 us
    all_gather x2, waiting for transfers between devices, over_seq(): return lax.all_gather(part, 'seq', axis=0, tiled=True)  53.9 us
    unnamed x524, local copies, waits for them, and re-layouts  42.1 us
    psum x1, waiting for transfers between devices, body(): hidden_out = hidden + lax.psum(last_rows, 'head')  35.7 us
    reduce_scatter x2, waiting for transfers between devices, body(): lax.psum_scatter(big[layer][:, 3 * inner_loc:3 * inner_loc + bc_all], 'he...  34.1 us
    all_gather x2, waiting for transfers between devices, body(): pieces = lax.all_gather(packed, 'seq')  33.8 us
  transfers between devices with their start and end apart: 18, of which 11 were waited for; matrix products, arithmetic and copies ran while one was open for 25% of the time, Pallas kernels for 0%

commit v1 on v0

--- a/solution.py
+++ b/solution.py
@@ -332,7 +332,9 @@
         )
         if layer == layers - 1:
             grad_part, hidden_out = lax.optimization_barrier((grad_part, hidden_out))
-        summed = lax.psum(with_rows(grad_part, shared), "head")
+        part_2 = with_rows(grad_part, shared)
+        shards = lax.all_gather(part_2, "head")
+        summed = jnp.sum(shards, axis=0)
         grad_hidden = grad_hidden + summed[:count]
         shared = summed[count:].reshape(-1)[: shared.shape[0]]
         big[layer] = lax.psum_scatter(

time: 834 us -> 964 us (1.16)
  waiting for transfers between devices: 382 us -> 498 us
  other arithmetic: 94.6 us -> 106 us
    all_gather x0 -> x2, waiting for transfers between devices: none -> 231 us  [body(): shards = lax.all_gather(part_2, 'head')]
    psum x2 -> x0, waiting for transfers between devices: 131 us -> none  [body(): summed = lax.psum(with_rows(grad_part, shared), 'head')]
    unnamed x16, waiting for transfers between devices: 25.4 us -> 47.6 us
    unnamed x524 -> x534, local copies, waits for them, and re-layouts: 42.1 us -> 43.1 us
  transfers between devices with their start and end apart: 18 -> 18, of which waited for: 11 -> 12; matrix products, arithmetic and copies ran while one was open for 25% -> 22% of each run, Pallas kernels for 0% -> 0%
where the time goes in v1:
time: 964 us; the launch traced here: 952 us
  waiting for transfers between devices  498 us (52%)
  matrix products  138 us (14%)
  local copies, waits for them, and re-layouts  129 us (13%)
  other arithmetic  106 us (11%)
  blocking collectives  52.5 us (5%)
  between operations  17.5 us (2%)
  starting transfers between devices  10.3 us (1%)
    all_gather x2, waiting for transfers between devices, body(): shards = lax.all_gather(part_2, 'head')  231 us
    dot_general x58, matrix products, product(): jnp.einsum(spec, left, right, precision=precision, preferred_element_type...  138 us
    psum x1, waiting for transfers between devices, body(): summed = lax.psum(with_rows(rows, squares), 'head')  67.9 us
    all_gather x2, waiting for transfers between devices, over_seq(): return lax.all_gather(part, 'seq', axis=0, tiled=True)  53.9 us
    unnamed x16, waiting for transfers between devices  47.6 us
    unnamed x534, local copies, waits for them, and re-layouts  43.1 us
    psum x1, waiting for transfers between devices, body(): hidden_out = hidden + lax.psum(last_rows, 'head')  36 us
    all_gather x2, waiting for transfers between devices, body(): pieces = lax.all_gather(packed, 'seq')  33.5 us
  transfers between devices with their start and end apart: 18, of which 12 were waited for; matrix products, arithmetic and copies ran while one was open for 22% of the time, Pallas kernels for 0%

profile of v1, /device:TPU:0, one launch (start us, length us, event | category | flops | bytes accessed | tf_op | source)
XLA Modules:
  0.0 951.6 jit_solution(13723462105524682835)
XLA Ops:
  10.9 15.7 %all_gather.41 = f32[2,101,256]{1,0,2:T(2,128)S(1)} all-gather(f32[2,101,64]{1,0,2:T(2,128)S(1)} %pad_maximum_fusion.19), channel_id=1, replica_groups=mesh['seq'=8,'head'=4] {'head'}, dimensions={2}, use_global_device_ids=true | all-gather | bytes 258560 | tf_op jit(solution)/shard_map/all_gather | solution.py:189
  34.5 4.4 slice_reduce_fusion.1
  42.0 25.5 %all-gather.13.cloned.1.call-done = f32[768,1292]{1,0:T(8,128)} async-done(((f32[96,1292]{1,0:T(8,128)}), f32[768,1292]{1,0:T(8,128)}) %all-gather.13.cloned.1.call-update) | async-done | bytes 3969040 | tf_op jit(solution)/shard_map/all_gather | solution.py:187
  107.6 17.7 %all-gather.21.cloned.1.call-done = f32[3136,128]{1,0:T(8,128)} async-done(((f32[392,128]{1,0:T(8,128)}), f32[3136,128]{1,0:T(8,128)}) %all-gather.21.cloned.1.call-update) | async-done | bytes 1605648 | tf_op jit(solution)/shard_map/all_gather | solution.py:259
  133.6 4.0 multiply_reduce_fusion.23
  137.6 28.4 %all-gather.15.cloned.1.call-done = f32[768,1536]{1,0:T(8,128)} async-done(((f32[96,1536]{1,0:T(8,128)}), f32[768,1536]{1,0:T(8,128)}) %all-gather.15.cloned.1.call-update) | async-done | bytes 4718608 | tf_op jit(solution)/shard_map/all_gather | solution.py:187
  165.9 3.7 fusion.94
  173.1 67.9 %all-reduce.56.cloned.1.call-done = f32[520,768]{1,0:T(8,128)} async-done(((f32[520,768]{1,0:T(8,128)}), f32[520,768]{1,0:T(8,128)}) %all-reduce.56.cloned.1.call-update) | async-done | bytes 1597456 | tf_op jit(solution)/shard_map/psum | solution.py:267
  250.5 3.9 fusion.18
  292.7 15.8 %all-gather.23.cloned.1.call-done = f32[3136,128]{1,0:T(8,128)} async-done(((f32[392,128]{1,0:T(8,128)}), f32[3136,128]{1,0:T(8,128)}) %all-gather.23.cloned.1.call-update) | async-done | bytes 1605648 | tf_op jit(solution)/shard_map/all_gather | solution.py:259
  324.9 3.9 multiply_reduce_fusion.22
  328.8 4.9 multiply_reduce_fusion.7
  334.3 12.4 %psum.29 = f32[2,512]{1,0:T(2,128)} all-reduce(f32[2,512]{1,0:T(2,128)} %pad_maximum_fusion.25), channel_id=1, replica_groups=mesh['seq'=8,'head'=4] {'head'}, use_global_device_ids=true, to_apply=%region_12.14 | all-reduce | flops 1024 | bytes 8192 | tf_op jit(solution)/shard_map/psum | solution.py:274
  350.7 3.4 multiply_reduce_fusion.18
  375.2 5.3 fusion.25
  420.8 4.9 fusion.89
  425.7 36.0 %all-reduce.58.cloned.1.call-done = f32[512,768]{1,0:T(8,128)} async-done(((f32[512,768]{1,0:T(8,128)}), f32[512,768]{1,0:T(8,128)}) %all-reduce.58.cloned.1.call-update) | async-done | bytes 1572880 | tf_op jit(solution)/shard_map/psum | solution.py:318
  461.7 8.3 multiply_reduce_fusion.4
  474.5 116.0 %all-gather.25.cloned.1.call-done = f32[2080,768]{1,0:T(8,128)} async-done(((f32[520,768]{1,0:T(8,128)}), f32[2080,768]{1,0:T(8,128)}) %all-gather.25.cloned.1.call-update) | async-done | bytes 6389776 | tf_op jit(solution)/shard_map/all_gather | solution.py:336
  590.5 4.6 reduce_sum.580
  621.5 5.9 copy.495
  633.0 5.2 fusion.27
  683.9 5.9 copy.493
  689.9 3.5 reduce-scatter.15.cloned.1.call-done
  695.5 3.7 fusion.96
  699.2 6.0 multiply_reduce_fusion.1
  706.8 43.9 %reduce-scatter.13.cloned.1.call-done = f32[96,1414]{1,0:T(8,128)} async-done(((f32[768,1414]{1,0:T(8,128)}), f32[96,1414]{1,0:T(8,128)}) %reduce-scatter.13.cloned.1.call-update) | async-done | bytes 542992
  763.9 8.4 reduce-scatter.11.cloned.1.call-done
  772.3 19.9 %reduce-scatter.9.cloned.1.call-done = f32[96,64]{0,1:T(8,128)} async-done(((f32[96,256]{0,1:T(8,128)}), f32[96,64]{0,1:T(8,128)}) %reduce-scatter.9.cloned.1.call-update) | async-done | bytes 24592 | tf_op jit(solution)/shard_map/reduce_scatter | solution.py:347
  793.6 115.1 %all-gather.27.cloned.1.call-done = f32[2080,768]{1,0:T(8,128)} async-done(((f32[520,768]{1,0:T(8,128)}), f32[2080,768]{1,0:T(8,128)}) %all-gather.27.cloned.1.call-update) | async-done | bytes 6389776 | tf_op jit(solution)/shard_map/all_gather | solution.py:336
  908.8 4.7 reduce_sum.695
  916.3 24.5 %psum.31 = f32[2,4370]{1,0:T(2,128)S(1)} all-reduce(f32[2,4370]{1,0:T(2,128)S(1)} %pad_maximum_fusion.21), channel_id=1, replica_groups=mesh['seq'=8,'head'=4] {'seq'}, use_global_device_ids=true, to_apply=%region_65.67 | all-reduce | flops 8740 | bytes 69920 | tf_op jit(solution)/shard_map/psum | solution.py:376
  (892 shorter events, 300.8 us)
Async XLA Ops:
  7.2 60.3 %all-gather.13.cloned.1.call-start = ((), (), s32[]{:S(2)}) async-start(), calls=%async_computation.4 | async-start | bytes 4866048 | tf_op jit(solution)/shard_map/all_gather | solution.py:187
  28.7 96.5 %all-gather.21.cloned.1.call-start = ((), (), s32[]{:S(2)}) async-start(), calls=%async_computation.12 | async-start | bytes 1806336 | tf_op jit(solution)/shard_map/all_gather | solution.py:259
  32.3 48.5 %copy-start.150 = (f32[640]{0:T(1024)}, f32[640]{0:T(1024)S(1)}, u32[]{:S(2)}) copy-start(f32[640]{0:T(1024)S(1)} %get-tuple-element.174) | copy-start | bytes 7684
  32.3 48.5 %copy-start.152 = (f32[640]{0:T(1024)}, f32[640]{0:T(1024)S(1)}, u32[]{:S(2)}) copy-start(f32[640]{0:T(1024)S(1)} %get-tuple-element.175) | copy-start | bytes 7684
  32.3 48.5 %copy-start.154 = (f32[640]{0:T(1024)}, f32[640]{0:T(1024)S(1)}, u32[]{:S(2)}) copy-start(f32[640]{0:T(1024)S(1)} %get-tuple-element.177) | copy-start | bytes 7684
  32.3 48.5 %copy-start.156 = (f32[640]{0:T(1024)}, f32[640]{0:T(1024)S(1)}, u32[]{:S(2)}) copy-start(f32[640]{0:T(1024)S(1)} %get-tuple-element.176) | copy-start | bytes 7684
  33.7 37.2 %copy-start.113 = (s32[384]{0:T(512)}, s32[384]{0:T(512)S(1)}, u32[]{:S(2)}) copy-start(s32[384]{0:T(512)S(1)} %add_select_fusion) | copy-start | bytes 4612
  40.4 37.9 %copy-start.208 = (f32[2]{0:T(128)}, f32[2]{0:T(128)S(1)}, u32[]{:S(2)}) copy-start(f32[2]{0:T(128)S(1)} %fusion.284) | copy-start | bytes 28
  41.9 36.4 %copy-start.140 = (f32[2,256]{1,0:T(2,128)}, f32[2,256]{1,0:T(2,128)S(1)}, u32[]{:S(2)}) copy-start(f32[2,256]{1,0:T(2,128)S(1)} %get-tuple-element.271) | copy-start | bytes 6148
  41.9 36.4 %copy-start.202 = (f32[2,256]{1,0:T(2,128)}, f32[2,256]{1,0:T(2,128)S(1)}, u32[]{:S(2)}) copy-start(f32[2,256]{1,0:T(2,128)S(1)} %get-tuple-element.272) | copy-start | bytes 6148
  42.0 38.9 %copy-start.128 = (f32[512]{0:T(512)}, f32[512]{0:T(512)S(1)}, u32[]{:S(2)}) copy-start(f32[512]{0:T(512)S(1)} %get-tuple-element.268) | copy-start | bytes 6148
  42.0 38.9 %copy-start.130 = (f32[512]{0:T(512)}, f32[512]{0:T(512)S(1)}, u32[]{:S(2)}) copy-start(f32[512]{0:T(512)S(1)} %get-tuple-element.269) | copy-start | bytes 6148
  42.0 38.9 %copy-start.133 = (f32[512]{0:T(512)}, f32[512]{0:T(512)S(1)}, u32[]{:S(2)}) copy-start(f32[512]{0:T(512)S(1)} %get-tuple-element.270) | copy-start | bytes 6148
  76.1 4.2 collective-permute-start
  94.3 71.7 %all-gather.15.cloned.1.call-start = ((), (), s32[]{:S(2)}) async-start(), calls=%async_computation.5 | async-start | bytes 5308416 | tf_op jit(solution)/shard_map/all_gather | solution.py:187
  97.2 143.8 %all-reduce.56.cloned.1.call-start = ((), (), s32[]{:S(2)}) async-start(), calls=%async_computation.6 | async-start | bytes 3194880 | tf_op jit(solution)/shard_map/psum | solution.py:267
  99.1 66.8 %copy-start.167 = (f32[384]{0:T(512)}, f32[384]{0:T(512)S(1)}, u32[]{:S(2)}) copy-start(f32[384]{0:T(512)S(1)} %get-tuple-element.185) | copy-start | bytes 4612
  99.9 283.5 %copy-start.120 = (pred[2,256,256]{2,1,0:T(8,128)(4,1)}, pred[2,256,256]{2,1,0:T(8,128)(4,1)S(1)}, u32[]{:S(2)}) copy-start(pred[2,256,256]{2,1,0:T(8,128)(4,1)S(1)} %compare_and_fusion) | copy-start | bytes 393220
  170.9 137.6 %all-gather.23.cloned.1.call-start = ((), (), s32[]{:S(2)}) async-start(), calls=%async_computation.13 | async-start | bytes 1806336 | tf_op jit(solution)/shard_map/all_gather | solution.py:259
  256.8 3.3 collective-permute-start.1
  278.3 111.8 %all-gather.17.cloned.1.call-start = ((), (), s32[]{:S(2)}) async-start(), calls=%async_computation.7 | async-start | bytes 1769472 | tf_op jit(solution)/shard_map/all_gather | solution.py:315
  362.6 99.1 %all-reduce.58.cloned.1.call-start = ((), (), s32[]{:S(2)}) async-start(), calls=%async_computation.8 | async-start | bytes 3145728 | tf_op jit(solution)/shard_map/psum | solution.py:318
  395.2 195.3 %all-gather.25.cloned.1.call-start = ((), (), s32[]{:S(2)}) async-start(), calls=%async_computation.14 | async-start | bytes 7987200 | tf_op jit(solution)/shard_map/all_gather | solution.py:336
  413.8 5.3 collective-permute-start.2
  474.3 173.2 %all-gather.19.cloned.1.call-start = ((), (), s32[]{:S(2)}) async-start(), calls=%async_computation.9 | async-start | bytes 1769472 | tf_op jit(solution)/shard_map/all_gather | solution.py:315
  611.4 82.0 %reduce-scatter.15.cloned.1.call-start = ((), (), s32[]{:S(2)}) async-start(), calls=%async_computation.17 | async-start | bytes 5308416
  627.5 123.2 %reduce-scatter.13.cloned.1.call-start = ((), (), s32[]{:S(2)}) async-start(), calls=%async_computation.16 | async-start | bytes 5308416
  672.1 4.7 collective-permute-start.3
  689.9 82.4 %reduce-scatter.11.cloned.1.call-start = ((), (), s32[]{:S(2)}) async-start(), calls=%async_computation.11 | async-start | bytes 163840 | tf_op jit(solution)/shard_map/reduce_scatter | solution.py:347
  695.1 97.1 %reduce-scatter.9.cloned.1.call-start = ((), (), s32[]{:S(2)}) async-start(), calls=%async_computation.10 | async-start | bytes 163840 | tf_op jit(solution)/shard_map/reduce_scatter | solution.py:347
  705.3 47.1 %slice-start.5 = ((f32[1,640]{1,0:T(1,128)}), f32[1,256]{1,0:T(1,128)S(1)}, s32[]{:S(2)}) async-start(f32[1,640]{1,0:T(1,128)} %copy-done.229), calls=%async_computation.23 | async-start | bytes 2048 | tf_op jit(solution)/shard_map/slice | solution.py:331
  752.3 156.4 %all-gather.27.cloned.1.call-start = ((), (), s32[]{:S(2)}) async-start(), calls=%async_computation.15 | async-start | bytes 7987200 | tf_op jit(solution)/shard_map/all_gather | solution.py:336
  (247 other events, 1032.0 us)
Sparse Core Ops, SparseCore 0:
  28.8 38.6 all-gather.12
  94.4 30.8 all-gather.20
  127.1 38.7 all-gather.14
  171.0 69.9 all-reduce.55
  278.4 30.0 all-gather.22
  362.7 22.7 all-gather.16
  395.4 66.2 all-reduce.57
  474.4 116.0 all-gather.24
  611.6 23.7 all-gather.18
  638.6 54.7 reduce-scatter.14
  696.9 53.7 reduce-scatter.12
  752.8 19.4 reduce-scatter.10
  774.5 17.6 reduce-scatter.8
  793.6 115.0 all-gather.26
